TPU v7x, 32 devices: a whole 2x2x4 slice. The times are simulated.
32 devices in a mesh: dp: 8 (over y, x, core), seq: 4 (over z).
Axes of the slice: x: 2, y: 2, z: 4, core: 2. Of those that a mesh axis runs over, the one named last changes fastest.
Arguments:
- block_input: float32 [32, 200, 768], P(('dp', 'seq')), may hold values from -6 to 6
- norm1_gain: bfloat16 [768], P('dp'), may hold values from 0.5 to 1.5
- norm1_bias: bfloat16 [768], P('dp'), may hold values from -1 to 1
- qkv_weight: bfloat16 [768, 2304], P('dp'), may hold values from -0.21875 to 0.21875
- query_bias: bfloat16 [768], P('dp'), may hold values from -1 to 1
- value_bias: bfloat16 [768], P('dp'), may hold values from -1 to 1
- out_weight: bfloat16 [768, 768], P('dp'), may hold values from -0.875 to 0.875
- out_bias: bfloat16 [768], P('dp'), may hold values from -1 to 1
- norm2_gain: bfloat16 [768], P('dp'), may hold values from 0.5 to 1.5
- norm2_bias: bfloat16 [768], P('dp'), may hold values from -1 to 1
- router_weight: bfloat16 [768, 32], P('dp'), may hold values from -0.21875 to 0.21875
- gate_weight: bfloat16 [32, 768, 2048], P('dp', None, 'seq'), may hold values from -0.21875 to 0.21875
- up_weight: bfloat16 [32, 768, 2048], P('dp', None, 'seq'), may hold values from -0.21875 to 0.21875
- down_weight: bfloat16 [32, 2048, 768], P('dp', 'seq'), may hold values from -2 to 2
- routes: int32 [32, 200, 2], P(('dp', 'seq')), may hold values from 0 to 31, all different within a row; in each aligned block of 200 rows (0 to 199, 200 to 399, ..., all dimensions but the last counted through in order) at most 14 rows name the same one
- key_mask: int32 [32, 200], P('dp'), may hold values from 0 to 1, as said below
- cotangent: float32 [32, 200, 768], P(('dp', 'seq')), may hold values from -6 to 6
Outputs:
- block_output: float32 [32, 200, 768], P(('dp', 'seq'))
- input_grad: float32 [32, 200, 768], P(('dp', 'seq'))
- norm1_gain_grad: float32 [768], P('dp')
- norm1_bias_grad: float32 [768], P('dp')
- qkv_weight_grad: float32 [768, 2304], P('dp')
- query_bias_grad: float32 [768], P('dp')
- value_bias_grad: float32 [768], P('dp')
- out_weight_grad: float32 [768, 768], P('dp')
- out_bias_grad: float32 [768], P('dp')
- norm2_gain_grad: float32 [768], P('dp')
- norm2_bias_grad: float32 [768], P('dp')
- router_weight_grad: float32 [768, 32], P('dp')
- gate_weight_grad: float32 [32, 768, 2048], P('dp', None, 'seq')
- up_weight_grad: float32 [32, 768, 2048], P('dp', None, 'seq')
- down_weight_grad: float32 [32, 2048, 768], P('dp', 'seq')
Inputs may be any that keep to these rules, and one draw needn't show every extreme that they name: `routes`: in each image, no expert is named by more than 14 tokens; a token's 2 experts differ. `key_mask`: each image has exactly 3 zeros, at positions that differ from image to image.
All inputs are finite; a program needn't handle non-finite values.
Results may differ from a plain program's by a relative error of at most 0.028.
Values may be sent and summed in bfloat16 or wider, within the bound.
No kernel may reach another device: no remote copies, remote signals or barrier semaphores. Data moves between devices by JAX's collectives and lax.ppermute only.
A program may use at most 192 MiB of HBM per device.

v0:
```python
import math
import jax
import jax.numpy as jnp
from jax import lax
from jax.sharding import PartitionSpec as P

HEAD = 64
EXPERTS = 32
TOP = 2
CAP = 14
epsilon = 1e-06


def normalize(values, norm_gain, norm_bias):
    average = jnp.mean(values, axis=-1, keepdims=True)
    centred = values - average
    variance = jnp.mean(centred * centred, axis=-1, keepdims=True)
    inverse = lax.rsqrt(variance + epsilon)
    unit_rows = centred * inverse
    scaled = unit_rows * norm_gain.astype(jnp.float32) + norm_bias.astype(jnp.float32)
    return (scaled, unit_rows, inverse)


def normalize_back(upstream, unit_rows, inverse, norm_gain):
    scaled = upstream * norm_gain.astype(jnp.float32)
    mean_term = jnp.mean(scaled, axis=-1, keepdims=True)
    proj_term = jnp.mean(scaled * unit_rows, axis=-1, keepdims=True)
    return inverse * (scaled - mean_term - unit_rows * proj_term)


def gelu_tanh(values):
    return jax.nn.gelu(values, approximate=True)


def to_heads(tensor):
    return lax.all_to_all(tensor, "seq", split_axis=2, concat_axis=0, tiled=True)


def to_tokens(tensor):
    return lax.all_to_all(tensor, "seq", split_axis=0, concat_axis=1, tiled=True)


def to_owners(tensor):
    return lax.all_to_all(tensor, "dp", split_axis=0, concat_axis=1, tiled=True)


def to_sources(tensor):
    return lax.all_to_all(tensor, "dp", split_axis=1, concat_axis=0, tiled=True)


def gather_rows(tensor):
    return lax.all_gather(tensor, "seq", axis=1, tiled=True)


def sum_partial(tensor):
    return lax.psum_scatter(
        tensor.astype(jnp.bfloat16), "seq", scatter_dimension=1, tiled=True
    ).astype(jnp.float32)


def compute_scores(head_q, head_k):
    scores = jnp.einsum("ihdq,ihdk->ihqk", head_q, head_k, preferred_element_type=jnp.float32)
    return scores * (1.0 / math.sqrt(HEAD))


def fill_slots(place_list, value_list):
    images = value_list[0].shape[0]
    width = value_list[0].shape[2]
    total = jnp.einsum(
        "sx,sd->xd", place_list[0][0], value_list[0][0], preferred_element_type=jnp.float32
    )
    for route_index in range(1, len(place_list)):
        total = total + jnp.einsum(
            "sx,sd->xd",
            place_list[route_index][0],
            value_list[route_index][0],
            preferred_element_type=jnp.float32,
        )
    per_image = [total.reshape(EXPERTS, CAP, width)]
    return jnp.stack(per_image, axis=1).astype(jnp.bfloat16).reshape(EXPERTS, images * CAP, width)


def read_slots(place_rows, returned, split_count):
    images = place_rows.shape[0]
    width = returned.shape[-1]
    shaped = returned.reshape(EXPERTS, split_count, images, CAP, width)
    total = jnp.dot(
        place_rows[0],
        shaped[:, 0, 0].reshape(EXPERTS * CAP, width),
        preferred_element_type=jnp.float32,
    )
    for half_index in range(1, split_count):
        total = total + jnp.dot(
            place_rows[0],
            shaped[:, half_index, 0].reshape(EXPERTS * CAP, width),
            preferred_element_type=jnp.float32,
        )
    per_image = [total]
    return jnp.stack(per_image, axis=0)


def per_device(
    block_input,
    norm1_gain,
    norm1_bias,
    qkv_weight,
    query_bias,
    value_bias,
    out_weight,
    out_bias,
    norm2_gain,
    norm2_bias,
    router_weight,
    gate_weight,
    up_weight,
    down_weight,
    routes,
    key_mask,
    cotangent,
):
    images, seq_rows, model_width = block_input.shape
    groups = lax.axis_size("seq")
    owners = lax.axis_size("dp")
    split_count = max(1, owners // EXPERTS)
    group_width = model_width // groups
    head_count = group_width // HEAD
    all_images = images * groups
    (
        gain_one,
        shift_one,
        qkv_full,
        query_full,
        value_full,
        out_full,
        obias_full,
        gain_two,
        shift_two,
        router_full,
    ) = (
        lax.all_gather(norm1_gain, "dp", axis=0, tiled=True),
        lax.all_gather(norm1_bias, "dp", axis=0, tiled=True),
        lax.all_gather(qkv_weight, "dp", axis=0, tiled=True),
        lax.all_gather(query_bias, "dp", axis=0, tiled=True),
        lax.all_gather(value_bias, "dp", axis=0, tiled=True),
        lax.all_gather(out_weight, "dp", axis=0, tiled=True),
        lax.all_gather(out_bias, "dp", axis=0, tiled=True),
        lax.all_gather(norm2_gain, "dp", axis=0, tiled=True),
        lax.all_gather(norm2_bias, "dp", axis=0, tiled=True),
        lax.all_gather(router_weight, "dp", axis=0, tiled=True),
    )
    normed_one, unit_one, inverse_one = normalize(block_input, gain_one, shift_one)
    normed_one = normed_one.astype(jnp.bfloat16)
    bias_row = jnp.concatenate(
        [
            query_full.astype(jnp.float32),
            jnp.zeros((model_width,), jnp.float32),
            value_full.astype(jnp.float32),
        ]
    )
    projected = (
        jnp.einsum("isd,df->ifs", normed_one, qkv_full, preferred_element_type=jnp.float32)
        + bias_row[None, :, None]
    ).astype(jnp.bfloat16)
    packed = projected.reshape(images, 3, groups, group_width, seq_rows)
    qkv_heads = to_heads(packed)
    head_q = qkv_heads[:, 0, 0].reshape(all_images, head_count, HEAD, seq_rows)
    head_k = qkv_heads[:, 1, 0].reshape(all_images, head_count, HEAD, seq_rows)
    head_v = qkv_heads[:, 2, 0].reshape(all_images, head_count, HEAD, seq_rows)
    key_open = key_mask.astype(jnp.float32)[:, None, None, :]
    scores = compute_scores(head_q, head_k)
    log_total = jnp.log(jnp.sum(jnp.exp(scores) * key_open, axis=-1))
    probs_b = (jnp.exp(scores - log_total[..., None]) * key_open).astype(jnp.bfloat16)
    mixed_heads = jnp.einsum("ihqk,ihdk->ihdq", probs_b, head_v, preferred_element_type=jnp.float32)
    mixed = to_tokens(mixed_heads.astype(jnp.bfloat16).reshape(all_images, group_width, seq_rows))
    residual_one = (
        block_input
        + jnp.einsum("ids,de->ise", mixed, out_full, preferred_element_type=jnp.float32)
        + obias_full.astype(jnp.float32)
    )
    normed_two, unit_two, inverse_two = normalize(residual_one, gain_two, shift_two)
    normed_two = normed_two.astype(jnp.bfloat16)
    logits = jnp.dot(normed_two, router_full, preferred_element_type=jnp.float32)
    expert_ids = jnp.arange(EXPERTS, dtype=jnp.int32)
    route_hot = (routes[..., None] == expert_ids).astype(jnp.int32)
    route_float = route_hot.astype(jnp.float32)
    logit_exp = jnp.exp(logits)
    router_probs = logit_exp / jnp.sum(logit_exp, axis=-1, keepdims=True)
    per_token = jnp.sum(route_hot, axis=2)
    earlier = jnp.cumsum(per_token, axis=1) - per_token
    slots = jnp.sum(route_hot * earlier[:, :, None, :], axis=-1)
    slot_ids = jnp.arange(EXPERTS * CAP, dtype=jnp.int32)
    places = []
    gates = []
    for route_index in range(TOP):
        target = routes[:, :, route_index] * CAP + slots[:, :, route_index]
        places.append((target[..., None] == slot_ids).astype(jnp.bfloat16))
        gates.append(jnp.sum(route_float[:, :, route_index] * router_probs, axis=-1))
    place_all = places[0]
    route_index = 1
    place_all = place_all + places[route_index]
    send_rows = fill_slots([place_all], [normed_two])
    send_rows = jnp.repeat(send_rows, split_count, axis=0)
    arrived = to_owners(send_rows)
    rows_all = gather_rows(arrived)
    gate_use, up_use, down_use = (gate_weight, up_weight, down_weight)
    gate_pre = jnp.einsum("prd,pdf->prf", rows_all, gate_use, preferred_element_type=jnp.float32)
    up_pre = jnp.einsum("prd,pdf->prf", rows_all, up_use, preferred_element_type=jnp.float32)
    activated, gelu_back = jax.vjp(gelu_tanh, gate_pre)
    hidden = (activated * up_pre).astype(jnp.bfloat16)
    partial_out = jnp.einsum("prf,pfd->prd", hidden, down_use, preferred_element_type=jnp.float32)
    piece_out = sum_partial(partial_out).astype(jnp.bfloat16)
    returned = to_sources(piece_out)
    expert_outs = [
        read_slots(places[route_index], returned, split_count) for route_index in range(TOP)
    ]
    block_output = residual_one
    for route_index in range(TOP):
        block_output = block_output + gates[route_index][..., None] * expert_outs[route_index]
    gate_grads = [
        jnp.sum(cotangent * expert_outs[route_index], axis=-1) for route_index in range(TOP)
    ]
    routed_grads = [
        (gates[route_index][..., None] * cotangent).astype(jnp.bfloat16)
        for route_index in range(TOP)
    ]
    send_grad = fill_slots(places, routed_grads)
    send_grad = jnp.repeat(send_grad, split_count, axis=0)
    arrived_grad = to_owners(send_grad)
    rows_grad = gather_rows(arrived_grad)
    hidden_grad = jnp.einsum(
        "prd,pfd->prf", rows_grad, down_use, preferred_element_type=jnp.float32
    )
    down_grad = jnp.einsum("prf,prd->pfd", hidden, rows_grad, preferred_element_type=jnp.float32)
    gate_pre_grad = gelu_back(hidden_grad * up_pre)[0].astype(jnp.bfloat16)
    up_pre_grad = (hidden_grad * activated).astype(jnp.bfloat16)
    gate_grad_w = jnp.einsum(
        "prd,prf->pdf", rows_all, gate_pre_grad, preferred_element_type=jnp.float32
    )
    up_grad_w = jnp.einsum(
        "prd,prf->pdf", rows_all, up_pre_grad, preferred_element_type=jnp.float32
    )
    rows_back = jnp.einsum(
        "prf,pdf->prd", gate_pre_grad, gate_use, preferred_element_type=jnp.float32
    ) + jnp.einsum("prf,pdf->prd", up_pre_grad, up_use, preferred_element_type=jnp.float32)
    rows_back = sum_partial(rows_back).astype(jnp.bfloat16)
    back_grad = to_sources(rows_back)
    moe_grad = read_slots(place_all, back_grad, split_count)
    spread = route_float[:, :, 0] * gate_grads[0][..., None]
    route_index = 1
    spread = spread + route_float[:, :, route_index] * gate_grads[route_index][..., None]
    logit_grad = (
        router_probs * (spread - jnp.sum(router_probs * spread, axis=-1, keepdims=True))
    ).astype(jnp.bfloat16)
    router_grad = jnp.einsum(
        "isd,ise->de", normed_two, logit_grad, preferred_element_type=jnp.float32
    )
    normed_two_grad = moe_grad + jnp.dot(
        logit_grad, router_full.T, preferred_element_type=jnp.float32
    )
    gain_two_grad = jnp.sum(normed_two_grad * unit_two, axis=(0, 1))
    shift_two_grad = jnp.sum(normed_two_grad, axis=(0, 1))
    residual_grad = cotangent + normalize_back(normed_two_grad, unit_two, inverse_two, gain_two)
    residual_b = residual_grad.astype(jnp.bfloat16)
    out_weight_grad = jnp.einsum(
        "ids,ise->de", mixed, residual_b, preferred_element_type=jnp.float32
    )
    out_bias_grad = jnp.sum(residual_grad, axis=(0, 1))
    mixed_grad = jnp.einsum(
        "ise,de->ids", residual_b, out_full, preferred_element_type=jnp.float32
    ).astype(jnp.bfloat16)
    mixed_grad = to_heads(mixed_grad.reshape(images, 1, groups, group_width, seq_rows))
    grad_heads = mixed_grad[:, 0, 0].reshape(all_images, head_count, HEAD, seq_rows)
    probs = jnp.exp(compute_scores(head_q, head_k) - log_total[..., None]) * key_open
    probs_grad = jnp.einsum(
        "ihdq,ihdk->ihqk", grad_heads, head_v, preferred_element_type=jnp.float32
    )
    row_term = jnp.sum(probs * probs_grad, axis=-1, keepdims=True)
    score_grad = (probs * (probs_grad - row_term) * (1.0 / math.sqrt(HEAD))).astype(jnp.bfloat16)
    value_grad = jnp.einsum(
        "ihqk,ihdq->ihdk", probs_b, grad_heads, preferred_element_type=jnp.float32
    ).astype(jnp.bfloat16)
    query_grad = jnp.einsum(
        "ihqk,ihdk->ihdq", score_grad, head_k, preferred_element_type=jnp.float32
    ).astype(jnp.bfloat16)
    key_grad = jnp.einsum(
        "ihqk,ihdq->ihdk", score_grad, head_q, preferred_element_type=jnp.float32
    ).astype(jnp.bfloat16)
    packed_grad = jnp.stack(
        [
            query_grad.reshape(all_images, group_width, seq_rows),
            key_grad.reshape(all_images, group_width, seq_rows),
            value_grad.reshape(all_images, group_width, seq_rows),
        ],
        axis=1,
    )
    tokens_grad = to_tokens(packed_grad.reshape(all_images, 3 * group_width, seq_rows))
    grouped_grad = tokens_grad.reshape(images, groups, 3, group_width, seq_rows)
    qkv_weight_grad = jnp.einsum(
        "isd,igtcs->dtgc", normed_one, grouped_grad, preferred_element_type=jnp.float32
    ).reshape(model_width, 3 * model_width)
    query_bias_grad = jnp.sum(grouped_grad[:, :, 0].astype(jnp.float32), axis=(0, 3)).reshape(
        model_width
    )
    value_bias_grad = jnp.sum(grouped_grad[:, :, 2].astype(jnp.float32), axis=(0, 3)).reshape(
        model_width
    )
    qkv_grouped = qkv_full.reshape(model_width, 3, groups, group_width)
    normed_one_grad = jnp.einsum(
        "igtcs,dtgc->isd", grouped_grad, qkv_grouped, preferred_element_type=jnp.float32
    )
    gain_one_grad = jnp.sum(normed_one_grad * unit_one, axis=(0, 1))
    shift_one_grad = jnp.sum(normed_one_grad, axis=(0, 1))
    input_grad = residual_grad + normalize_back(normed_one_grad, unit_one, inverse_one, gain_one)
    shares = (
        lax.psum_scatter(gain_one_grad, "dp", scatter_dimension=0, tiled=True),
        lax.psum_scatter(shift_one_grad, "dp", scatter_dimension=0, tiled=True),
        lax.psum_scatter(qkv_weight_grad, "dp", scatter_dimension=0, tiled=True),
        lax.psum_scatter(query_bias_grad, "dp", scatter_dimension=0, tiled=True),
        lax.psum_scatter(value_bias_grad, "dp", scatter_dimension=0, tiled=True),
        lax.psum_scatter(out_weight_grad, "dp", scatter_dimension=0, tiled=True),
        lax.psum_scatter(out_bias_grad, "dp", scatter_dimension=0, tiled=True),
        lax.psum_scatter(gain_two_grad, "dp", scatter_dimension=0, tiled=True),
        lax.psum_scatter(shift_two_grad, "dp", scatter_dimension=0, tiled=True),
        lax.psum_scatter(router_grad, "dp", scatter_dimension=0, tiled=True),
    )
    (
        gain_one_sum,
        shift_one_sum,
        qkv_sum,
        query_sum,
        value_sum,
        out_sum,
        obias_sum,
        gain_two_sum,
        shift_two_sum,
        router_sum,
    ) = (
        lax.psum(shares[0].astype(jnp.bfloat16), "seq").astype(jnp.float32),
        lax.psum(shares[1].astype(jnp.bfloat16), "seq").astype(jnp.float32),
        lax.psum(shares[2].astype(jnp.bfloat16), "seq").astype(jnp.float32),
        lax.psum(shares[3].astype(jnp.bfloat16), "seq").astype(jnp.float32),
        lax.psum(shares[4].astype(jnp.bfloat16), "seq").astype(jnp.float32),
        lax.psum(shares[5].astype(jnp.bfloat16), "seq").astype(jnp.float32),
        lax.psum(shares[6].astype(jnp.bfloat16), "seq").astype(jnp.float32),
        lax.psum(shares[7].astype(jnp.bfloat16), "seq").astype(jnp.float32),
        lax.psum(shares[8].astype(jnp.bfloat16), "seq").astype(jnp.float32),
        lax.psum(shares[9].astype(jnp.bfloat16), "seq").astype(jnp.float32),
    )
    return (
        block_output,
        input_grad,
        gain_one_sum,
        shift_one_sum,
        qkv_sum,
        query_sum,
        value_sum,
        out_sum,
        obias_sum,
        gain_two_sum,
        shift_two_sum,
        router_sum,
        gate_grad_w,
        up_grad_w,
        down_grad,
    )


def solution(mesh):
    in_specs = (
        P(("dp", "seq"), None, None),
        P("dp"),
        P("dp"),
        P("dp", None),
        P("dp"),
        P("dp"),
        P("dp", None),
        P("dp"),
        P("dp"),
        P("dp"),
        P("dp", None),
        P("dp", None, "seq"),
        P("dp", None, "seq"),
        P("dp", "seq", None),
        P(("dp", "seq"), None, None),
        P("dp", None),
        P(("dp", "seq"), None, None),
    )
    out_specs = (
        P(("dp", "seq"), None, None),
        P(("dp", "seq"), None, None),
        P("dp"),
        P("dp"),
        P("dp", None),
        P("dp"),
        P("dp"),
        P("dp", None),
        P("dp"),
        P("dp"),
        P("dp"),
        P("dp", None),
        P("dp", None, "seq"),
        P("dp", None, "seq"),
        P("dp", "seq", None),
    )
    return jax.shard_map(
        per_device, mesh=mesh, in_specs=in_specs, out_specs=out_specs, check_vma=False
    )
```

profile of v0, /device:TPU:0, one launch (start us, length us, event | category | flops | bytes accessed | tf_op | source)
XLA Modules:
  0.0 666.3 jit_solution(9371943102563862651)
XLA Ops:
  15.9 26.9 %all-reduce.16 = (bf16[768]{0:T(1024)(128)(2,1)S(1)}, bf16[768]{0:T(1024)(128)(2,1)S(1)}, bf16[768]{0:T(1024)(128)(2,1)S(1)}, bf16[768]{0:T(1024)(128)(2,1)S(1)}...) all-reduce(bf16[768]{0:T(1024)(128)(2,1)S(1)} %dynamic-update-slice, ...), channel_id=1, replica_groups=mesh['dp'=8,'seq'=4] {'dp'}, use_global_device_ids=true, to_apply=%add.4 | all-reduce | flops 5376 | bytes 21504
  46.7 4.1 fusion.10
  50.8 3.8 reshape.635
  54.6 3.4 copy.98
  58.0 4.6 all-to-all-start
  65.8 25.9 %all-to-all-done = bf16[1,3,4,192,200]{4,3,1,0,2:T(8,128)(2,1)} async-done(((bf16[1,3,4,192,200]{4,3,1,0,2:T(8,128)(2,1)}), bf16[1,3,4,192,200]{4,3,1,0,2:T(8,128)(2,1)}, u32[]{:S(2)}, u32[]{:S(2)}) %all-to-all-start) | async-done | bytes 921632 | tf_op jit(solution)/shard_map/all_to_all | solution.py:36
  95.7 4.3 convolution_convert_fusion.3
  100.0 3.5 all-to-all-start.1
  108.2 6.5 all-to-all-done.1
  118.7 15.0 %all_to_all.111 = bf16[32,14,768]{2,1,0:T(8,128)(2,1)S(1)} all-to-all(bf16[32,14,768]{2,1,0:T(8,128)(2,1)S(1)} %copy.104), channel_id=1, replica_groups=mesh['dp'=8,'seq'=4] {'dp'}, dimensions={0} | all-to-all | bytes 1376256 | tf_op jit(solution)/shard_map/all_to_all | solution.py:44
  135.3 54.0 %all-gather.10.cloned.1.call-done = bf16[4,448,768]{2,1,0:T(8,128)(2,1)} async-done(((bf16[4,112,768]{2,1,0:T(8,128)(2,1)}), bf16[4,448,768]{2,1,0:T(8,128)(2,1)}) %all-gather.10.cloned.1.call-update) | async-done | bytes 2752528 | tf_op jit(solution)/shard_map/all_gather | solution.py:52
  189.3 4.5 fusion.128
  193.8 3.8 multiply_convert_fusion.1
  198.9 3.1 convolution_convert_fusion
  202.0 53.2 %reduce-scatter.10.cloned.1.call-done = bf16[4,112,768]{2,1,0:T(8,128)(2,1)} async-done(((bf16[4,448,768]{2,1,0:T(8,128)(2,1)}), bf16[4,112,768]{2,1,0:T(8,128)(2,1)}) %reduce-scatter.10.cloned.1.call-update) | async-done | bytes 688144 | tf_op jit(solution)/shard_map/reduce_scatter | solution.py:56
  255.2 2.3 copy.107
  257.5 4.2 all-to-all-start.3
  261.8 14.8 %all-gather = bf16[8,96,32]{1,2,0:T(8,128)(2,1)S(1)} all-gather(bf16[1,96,32]{1,2,0:T(8,128)(2,1)} %bitcast.285), channel_id=1, replica_groups=mesh['dp'=8,'seq'=4] {'dp'}, dimensions={0}, use_global_device_ids=true | all-gather | bytes 55296 | tf_op jit(solution)/shard_map/all_gather | solution.py:149
  279.4 2.4 fusion.126
  288.3 2.5 fusion.52
  295.5 16.0 %all_to_all.112 = bf16[32,14,768]{2,1,0:T(8,128)(2,1)S(1)} all-to-all(bf16[32,14,768]{2,1,0:T(8,128)(2,1)} %convert_element_type.299), channel_id=1, replica_groups=mesh['dp'=8,'seq'=4] {'dp'}, dimensions={0} | all-to-all | bytes 1376256 | tf_op jit(solution)/shard_map/all_to_all | solution.py:44
  313.3 54.3 %all-gather.12.cloned.1.call-done = bf16[4,448,768]{2,1,0:T(8,128)(2,1)} async-done(((bf16[4,112,768]{2,1,0:T(8,128)(2,1)}), bf16[4,448,768]{2,1,0:T(8,128)(2,1)}) %all-gather.12.cloned.1.call-update) | async-done | bytes 2752528 | tf_op jit(solution)/shard_map/all_gather | solution.py:52
  367.7 7.1 %multiply_convert_fusion = (bf16[4,448,512]{2,1,0:T(8,128)(2,1)S(1)}, bf16[4,448,512]{2,1,0:T(8,128)(2,1)S(1)}) fusion(f32[4,448,512]{2,1,0:T(8,128)} %copy-done.23, f32[4,448,512]{2,1,0:T(8,128)} %get-tuple-element.114, bf16[4,448,768]{2,1,0:T(8,128)(2,1)} %all-gather.12.cloned.1.call-done, bf16[4,512,768]{2,1,0:T(8,128)(2,1)S(1)} %copy-done), kind=kOutput, calls=%fused_computation.14 | convolution fusion | flops 1431306240 | bytes 16908288 | tf_op jit(solution)/shard_map/prd,pfd->prf/dot_general | solution.py:230
  378.0 3.3 add_convert_fusion
  381.4 53.2 %reduce-scatter.12.cloned.1.call-done = bf16[4,112,768]{2,1,0:T(8,128)(2,1)} async-done(((bf16[4,448,768]{2,1,0:T(8,128)(2,1)}), bf16[4,112,768]{2,1,0:T(8,128)(2,1)}) %reduce-scatter.12.cloned.1.call-update) | async-done | bytes 688144 | tf_op jit(solution)/shard_map/reduce_scatter | solution.py:56
  434.5 2.3 copy.111
  436.8 3.7 all-to-all-start.5
  442.9 9.0 %all-to-all-done.5 = bf16[4,112,768]{2,0,1:T(4,128)(2,1)S(1)} async-done(((bf16[4,112,768]{2,0,1:T(4,128)(2,1)}), bf16[4,112,768]{2,0,1:T(4,128)(2,1)S(1)}, u32[]{:S(2)}, u32[]{:S(2)}) %all-to-all-start.5) | async-done | bytes 688160 | tf_op jit(solution)/shard_map/all_to_all | solution.py:48
  455.2 2.5 fusion.44
  463.6 3.5 all-to-all-start.6
  467.3 2.8 fusion.14
  470.2 6.1 all-to-all-done.6
  477.0 4.3 convolution_convert_fusion.2
  483.0 4.0 fusion.33
  486.9 4.2 fusion.30
  493.3 26.0 %all_to_all.113 = bf16[4,576,200]{1,2,0:T(8,128)(2,1)} all-to-all(bf16[4,576,200]{1,2,0:T(8,128)(2,1)S(1)} %copy.120), channel_id=1, replica_groups=mesh['dp'=8,'seq'=4] {'seq'}, dimensions={0} | all-to-all | bytes 1843200 | tf_op jit(solution)/shard_map/all_to_all | solution.py:40
  522.1 3.4 copy.124
  525.5 8.0 %copy.134 = f32[768,2304]{1,0:T(8,128)} copy(f32[768,2304]{0,1:T(8,128)} %bitcast.243) | data formatting | bytes 14155776
  534.5 5.9 copy.122
  541.3 6.8 %fusion.132 = f32[4,768,512]{2,1,0:T(8,128)} fusion(bf16[4,448,768]{2,1,0:T(8,128)(2,1)S(1)} %copy-done.3, bf16[4,448,512]{2,1,0:T(8,128)(2,1)} %copy-done.16), kind=kOutput, calls=%fused_computation.185 | convolution fusion | flops 1409286144 | bytes 10878976 | tf_op jit(solution)/shard_map/prd,prf->pdf/dot_general | solution.py:236
  548.0 4.6 fusion.133
  552.6 4.6 fusion.134
  557.8 3.8 fusion.43
  563.3 38.4 %reduce-scatter.16.cloned.1.call-done = f32[96,2304]{1,0:T(8,128)} async-done(((f32[768,2304]{1,0:T(8,128)}), f32[96,2304]{1,0:T(8,128)}) %reduce-scatter.16.cloned.1.call-update) | async-done | bytes 884752
  601.6 2.2 copy.135
  605.3 23.7 %all-reduce.15 = (bf16[768]{0:T(1024)(128)(2,1)S(1)}, bf16[768]{0:T(1024)(128)(2,1)S(1)}, bf16[768]{0:T(1024)(128)(2,1)S(1)}, bf16[768]{0:T(1024)(128)(2,1)S(1)}...) all-reduce(f32[768]{0:T(1024)S(1)} %get-tuple-element.62, ...), channel_id=4, replica_groups=mesh['dp'=8,'seq'=4] {'dp'}, use_global_device_ids=true, to_apply=%region_23.24.clone | all-reduce | flops 5376 | bytes 32256
  629.6 19.1 %all-reduce.17 = (bf16[96]{0:T(256)(128)(2,1)S(1)}, bf16[96]{0:T(256)(128)(2,1)S(1)}, bf16[96]{0:T(256)(128)(2,1)S(1)}, bf16[96]{0:T(256)(128)(2,1)S(1)}, bf16[9...) all-reduce(bf16[96]{0:T(256)(128)(2,1)S(1)} %dynamic-slice.34, ...), channel_id=1, replica_groups=mesh['dp'=8,'seq'=4] {'seq'}, use_global_device_ids=true, to_apply=%region_24.25 | all-reduce | flops 3744 | bytes 14976 | tf_op jit(solution)/shard_map/psum | solution.py:338
  652.9 2.5 fusion.47
  (289 shorter events, 81.8 us)
Async XLA Ops:
  7.2 191.7 %copy-start = (bf16[4,512,768]{2,1,0:T(8,128)(2,1)S(1)}, bf16[4,512,768]{2,1,0:T(8,128)(2,1)}, u32[]{:S(2)}) copy-start(bf16[4,512,768]{2,1,0:T(8,128)(2,1)} %param.30) | copy-start | bytes 9437188
  7.2 39.5 %all-gather.6.cloned.1.call-start = ((), (), s32[]{:S(2)}) async-start(), calls=%async_computation.13 | async-start | bytes 3981312 | tf_op jit(solution)/shard_map/all_gather | solution.py:142
  42.8 7.9 %copy-start.43 = (f32[768]{0:T(1024)}, f32[768]{0:T(1024)S(1)}, u32[]{:S(2)}) copy-start(f32[768]{0:T(1024)S(1)} %convert_element_type.274) | copy-start | bytes 9220
  44.1 6.7 %copy-start.45 = (f32[200]{0:T(256)}, f32[200]{0:T(256)S(1)}, u32[]{:S(2)}) copy-start(f32[200]{0:T(256)S(1)} %broadcast_multiply_fusion.5) | copy-start | bytes 2404
  54.6 8.8 %copy-start.42 = (s32[1,200,2]{1,2,0:T(2,128)S(1)}, s32[1,200,2]{1,2,0:T(2,128)}, u32[]{:S(2)}) copy-start(s32[1,200,2]{1,2,0:T(2,128)} %param.31) | copy-start | bytes 4804
  54.6 9.4 %copy-start.72 = (s32[4,200]{1,0:T(4,128)S(1)}, s32[4,200]{1,0:T(4,128)}, u32[]{:S(2)}) copy-start(s32[4,200]{1,0:T(4,128)} %param.32) | copy-start | bytes 9604
  58.0 33.6 %all-to-all-start = ((bf16[1,3,4,192,200]{4,3,1,0,2:T(8,128)(2,1)}), bf16[1,3,4,192,200]{4,3,1,0,2:T(8,128)(2,1)}, u32[]{:S(2)}, u32[]{:S(2)}) async-start(bf16[1,3,4,192,200]{4,3,1,0,2:T(8,128)(2,1)} %copy.98), calls=%async_computation | async-start | bytes 2359296 | tf_op jit(solution)/shard_map/all_to_all | solution.py:36
  62.6 45.6 %all-gather.8.cloned.1.call-start = ((), (), s32[]{:S(2)}) async-start(), calls=%async_computation.14 | async-start | bytes 1327104 | tf_op jit(solution)/shard_map/all_gather | solution.py:145
  64.0 31.7 %copy-start.73 = (f32[4,200]{1,0:T(4,128)}, f32[4,200]{1,0:T(4,128)S(1)}, u32[]{:S(2)}) copy-start(f32[4,200]{1,0:T(4,128)S(1)} %convert_element_type.280) | copy-start | bytes 9604
  93.0 7.0 %copy-start.33 = (bf16[4,1,1,192,200]{4,3,1,0,2:T(8,128)(2,1)}, bf16[4,1,1,192,200]{4,3,1,0,2:T(8,128)(2,1)S(1)}, u32[]{:S(2)}) copy-start(bf16[4,1,1,192,200]{4,3,1,0,2:T(8,128)(2,1)S(1)} %get-tuple-element.105) | copy-start | bytes 921604
  100.0 14.7 %all-to-all-start.1 = ((bf16[4,192,200]{2,1,0:T(8,128)(2,1)}), bf16[4,192,200]{2,1,0:T(8,128)(2,1)S(1)}, u32[]{:S(2)}, u32[]{:S(2)}) async-start(bf16[4,192,200]{2,1,0:T(8,128)(2,1)} %bitcast.269), calls=%async_computation.1 | async-start | bytes 786432 | tf_op jit(solution)/shard_map/all_to_all | solution.py:40
  103.5 85.8 %all-gather.10.cloned.1.call-start = ((), (), s32[]{:S(2)}) async-start(), calls=%async_computation.15 | async-start | bytes 3440640 | tf_op jit(solution)/shard_map/all_gather | solution.py:52
  116.7 17.0 %copy-start.6 = (f32[1,200,768]{2,1,0:T(8,128)}, f32[1,200,768]{2,1,0:T(8,128)S(1)}, u32[]{:S(2)}) copy-start(f32[1,200,768]{2,1,0:T(8,128)S(1)} %get-tuple-element.112) | copy-start | bytes 1843204
  135.0 120.2 %reduce-scatter.10.cloned.1.call-start = ((), (), s32[]{:S(2)}) async-start(), calls=%async_computation.16 | async-start | bytes 3440640 | tf_op jit(solution)/shard_map/reduce_scatter | solution.py:56
  257.5 24.3 %all-to-all-start.3 = ((bf16[4,112,768]{2,0,1:T(4,128)(2,1)}), bf16[4,112,768]{2,0,1:T(4,128)(2,1)}, u32[]{:S(2)}, u32[]{:S(2)}) async-start(bf16[4,112,768]{2,0,1:T(4,128)(2,1)} %copy.107), calls=%async_computation.4 | async-start | bytes 1376256 | tf_op jit(solution)/shard_map/all_to_all | solution.py:48
  261.7 106.0 %all-gather.12.cloned.1.call-start = ((), (), s32[]{:S(2)}) async-start(), calls=%async_computation.17 | async-start | bytes 3440640 | tf_op jit(solution)/shard_map/all_gather | solution.py:52
  283.9 7.6 %copy-start.50 = (s32[1,200,1]{1,2,0:T(1,128)S(1)}, s32[1,200,1]{1,2,0:T(1,128)}, u32[]{:S(2)}) copy-start(s32[1,200,1]{1,2,0:T(1,128)} %get-tuple-element.107) | copy-start | bytes 2404
  285.9 5.5 copy-start.10
  312.8 121.8 %reduce-scatter.12.cloned.1.call-start = ((), (), s32[]{:S(2)}) async-start(), calls=%async_computation.18 | async-start | bytes 3440640 | tf_op jit(solution)/shard_map/reduce_scatter | solution.py:56
  367.7 7.1 %copy-start.8 = (bf16[4,768,512]{2,1,0:T(8,128)(2,1)S(1)}, bf16[4,768,512]{2,1,0:T(8,128)(2,1)}, u32[]{:S(2)}) copy-start(bf16[4,768,512]{2,1,0:T(8,128)(2,1)} %param.28) | copy-start | bytes 9437188
  381.3 59.3 %copy-start.36 = (f32[1,200,2,32]{1,3,2,0:T(8,128)S(1)}, f32[1,200,2,32]{1,3,2,0:T(8,128)}, u32[]{:S(2)}) copy-start(f32[1,200,2,32]{1,3,2,0:T(8,128)} %convert_convert_fusion) | copy-start | bytes 153604
  381.3 59.3 %copy-start.40 = (f32[200,32]{0,1:T(8,128)S(1)}, f32[200,32]{0,1:T(8,128)}, u32[]{:S(2)}) copy-start(f32[200,32]{0,1:T(8,128)} %get-tuple-element.117) | copy-start | bytes 76804
  381.3 59.3 %copy-start.66 = (f32[200]{0:T(256)S(1)}, f32[200]{0:T(256)}, u32[]{:S(2)}) copy-start(f32[200]{0:T(256)} %get-tuple-element.116) | copy-start | bytes 2404
  381.3 59.3 %copy-start.68 = (f32[200]{0:T(256)S(1)}, f32[200]{0:T(256)}, u32[]{:S(2)}) copy-start(f32[200]{0:T(256)} %copy-done.67) | copy-start | bytes 2404
  381.3 59.3 %copy-start.70 = (f32[200]{0:T(256)S(1)}, f32[200]{0:T(256)}, u32[]{:S(2)}) copy-start(f32[200]{0:T(256)} %copy-done.69) | copy-start | bytes 2404
  381.3 59.3 %copy-start.75 = (f32[200]{0:T(256)S(1)}, f32[200]{0:T(256)}, u32[]{:S(2)}) copy-start(f32[200]{0:T(256)} %get-tuple-element.72) | copy-start | bytes 2404
  381.3 59.3 %copy-start.27 = (bf16[1,200,768]{2,1,0:T(8,128)(2,1)S(1)}, bf16[1,200,768]{2,1,0:T(8,128)(2,1)}, u32[]{:S(2)}) copy-start(bf16[1,200,768]{2,1,0:T(8,128)(2,1)} %copy-done.26) | copy-start | bytes 921604
  381.4 60.5 %copy-start.37 = (bf16[768,32]{0,1:T(8,128)(2,1)S(1)}, bf16[768,32]{0,1:T(8,128)(2,1)}, u32[]{:S(2)}) copy-start(bf16[768,32]{0,1:T(8,128)(2,1)} %reshape.675) | copy-start | bytes 147460
  436.8 15.1 %all-to-all-start.5 = ((bf16[4,112,768]{2,0,1:T(4,128)(2,1)}), bf16[4,112,768]{2,0,1:T(4,128)(2,1)S(1)}, u32[]{:S(2)}, u32[]{:S(2)}) async-start(bf16[4,112,768]{2,0,1:T(4,128)(2,1)} %copy.111), calls=%async_computation.7 | async-start | bytes 1376256 | tf_op jit(solution)/shard_map/all_to_all | solution.py:48
  440.5 14.6 %copy-start.7 = (f32[1,200,768]{2,1,0:T(8,128)S(1)}, f32[1,200,768]{2,1,0:T(8,128)}, u32[]{:S(2)}) copy-start(f32[1,200,768]{2,1,0:T(8,128)} %copy-done.6) | copy-start | bytes 1843204
  440.5 14.6 %copy-start.48 = (f32[200]{0:T(256)S(1)}, f32[200]{0:T(256)}, u32[]{:S(2)}) copy-start(f32[200]{0:T(256)} %copy-done.47) | copy-start | bytes 2404
  440.5 14.6 %copy-start.51 = (s32[1,200,1]{1,2,0:T(1,128)S(1)}, s32[1,200,1]{1,2,0:T(1,128)}, u32[]{:S(2)}) copy-start(s32[1,200,1]{1,2,0:T(1,128)} %get-tuple-element.107) | copy-start | bytes 2404
  440.5 14.6 %copy-start.58 = (s32[1,200,1]{1,2,0:T(1,128)S(1)}, s32[1,200,1]{1,2,0:T(1,128)}, u32[]{:S(2)}) copy-start(s32[1,200,1]{1,2,0:T(1,128)} %get-tuple-element.108) | copy-start | bytes 2404
  440.5 99.9 %reduce-scatter.18.cloned.1.call-start = ((), (), s32[]{:S(2)}) async-start(), calls=%async_computation.21 | async-start | bytes 442368
  441.8 119.8 %reduce-scatter.14.cloned.1.call-start = ((), (), s32[]{:S(2)}) async-start(), calls=%async_computation.19 | async-start | bytes 2654208 | tf_op jit(solution)/shard_map/reduce_scatter | solution.py:320
  463.6 12.6 %all-to-all-start.6 = ((bf16[1,1,4,192,200]{4,3,1,0,2:T(8,128)(2,1)}), bf16[1,1,4,192,200]{4,3,1,0,2:T(8,128)(2,1)S(1)}, u32[]{:S(2)}, u32[]{:S(2)}) async-start(bf16[1,1,4,192,200]{4,3,1,0,2:T(8,128)(2,1)} %bitcast.52), calls=%async_computation.8 | async-start | bytes 786432 | tf_op jit(solution)/shard_map/all_to_all | solution.py:36
  467.1 134.5 %reduce-scatter.16.cloned.1.call-start = ((), (), s32[]{:S(2)}) async-start(), calls=%async_computation.20 | async-start | bytes 7962624
  493.2 27.6 %copy-start.4 = (f32[1,200,768]{2,1,0:T(8,128)S(1)}, f32[1,200,768]{2,1,0:T(8,128)}, u32[]{:S(2)}) copy-start(f32[1,200,768]{2,1,0:T(8,128)} %param.17) | copy-start | bytes 1843204
  493.2 27.6 %copy-start.44 = (f32[768]{0:T(1024)S(1)}, f32[768]{0:T(1024)}, u32[]{:S(2)}) copy-start(f32[768]{0:T(1024)} %copy-done.43) | copy-start | bytes 9220
  493.2 27.6 %copy-start.46 = (f32[200]{0:T(256)S(1)}, f32[200]{0:T(256)}, u32[]{:S(2)}) copy-start(f32[200]{0:T(256)} %copy-done.45) | copy-start | bytes 2404
  493.2 27.6 %copy-start.60 = (f32[200]{0:T(256)S(1)}, f32[200]{0:T(256)}, u32[]{:S(2)}) copy-start(f32[200]{0:T(256)} %copy-done.59) | copy-start | bytes 2404
  533.5 121.8 %all-reduce.21.cloned.1.call-start = ((), (), s32[]{:S(2)}) async-start(), calls=%async_computation.22 | async-start | bytes 1474560 | tf_op jit(solution)/shard_map/psum | solution.py:340
  534.4 6.8 %copy-start.3 = (bf16[4,448,768]{2,1,0:T(8,128)(2,1)S(1)}, bf16[4,448,768]{2,1,0:T(8,128)(2,1)}, u32[]{:S(2)}) copy-start(bf16[4,448,768]{2,1,0:T(8,128)(2,1)} %all-gather.10.cloned.1.call-done) | copy-start | bytes 8257540
  541.2 6.8 %copy-start.15 = (bf16[4,448,512]{2,1,0:T(8,128)(2,1)S(1)}, bf16[4,448,512]{2,1,0:T(8,128)(2,1)}, u32[]{:S(2)}) copy-start(bf16[4,448,512]{2,1,0:T(8,128)(2,1)} %copy-done.14) | copy-start | bytes 5505028
  561.6 43.7 %copy-start.52 = (f32[768]{0:T(1024)S(1)}, f32[768]{0:T(1024)}, u32[]{:S(2)}) copy-start(f32[768]{0:T(1024)} %get-tuple-element.60) | copy-start | bytes 9220
  561.6 43.7 %copy-start.53 = (f32[768]{0:T(1024)S(1)}, f32[768]{0:T(1024)}, u32[]{:S(2)}) copy-start(f32[768]{0:T(1024)} %get-tuple-element.66) | copy-start | bytes 9220
  561.6 43.7 %copy-start.54 = (f32[768]{0:T(1024)S(1)}, f32[768]{0:T(1024)}, u32[]{:S(2)}) copy-start(f32[768]{0:T(1024)} %get-tuple-element.99) | copy-start | bytes 9220
  603.9 55.3 %copy-start.1 = (bf16[4,512,768]{2,1,0:T(8,128)(2,1)S(1)}, bf16[4,512,768]{2,1,0:T(8,128)(2,1)}, u32[]{:S(2)}) copy-start(bf16[4,512,768]{2,1,0:T(8,128)(2,1)} %param.30) | copy-start | bytes 9437188
  (43 other events, 135.6 us)
Sparse Core Ops, SparseCore 0:
  9.9 36.7 all-gather.5
  65.3 24.3 all-gather.7
  135.1 54.1 all-gather.9
  202.1 53.0 reduce-scatter.9
  312.9 54.7 all-gather.11
  381.5 53.0 reduce-scatter.11
  444.4 34.0 reduce-scatter.17
  481.8 42.4 reduce-scatter.13
  533.7 67.9 reduce-scatter.15
  604.5 43.2 all-reduce.20
where the time goes:
time: 675 us; the launch traced here: 666 us
  waiting for transfers between devices  303 us (45%)
  blocking collectives  142 us (21%)
  matrix products  89.5 us (13%)
  local copies, waits for them, and re-layouts  68.6 us (10%)
  other arithmetic  25.7 us (4%)
  starting transfers between devices  20.9 us (3%)
  between operations  16.6 us (2%)
    all_gather x2, waiting for transfers between devices, gather_rows(): return lax.all_gather(tensor, 'seq', axis=1, tiled=True)  108 us
    reduce_scatter x2, waiting for transfers between devices, sum_partial(): lax.psum_scatter(tensor.astype(jnp.bfloat16), 'seq', scatter_dimension=1,...  106 us
    unnamed x2, blocking collectives  50.7 us
    unnamed x12, waiting for transfers between devices  39.9 us
    all_to_all x2, waiting for transfers between devices, to_heads(): lax.all_to_all(tensor, 'seq', split_axis=2, concat_axis=0, tiled=True)  31.9 us
    all_to_all x2, blocking collectives, to_owners(): return lax.all_to_all(tensor, 'dp', split_axis=0, concat_axis=1, tiled=True)  31 us
    unnamed x180, local copies, waits for them, and re-layouts  29.5 us
    all_to_all x1, blocking collectives, to_tokens(): lax.all_to_all(tensor, 'seq', split_axis=0, concat_axis=1, tiled=True)  26 us
  transfers between devices with their start and end apart: 15, of which 10 were waited for; matrix products, arithmetic and copies ran while one was open for 17% of the time, Pallas kernels for 0%

commit v1 on v0

--- a/solution.py
+++ b/solution.py
@@ -9,6 +9,27 @@
 TOP = 2
 CAP = 14
 epsilon = 1e-06
+
+
+def joined_along(pieces, dim):
+    pieces = jnp.moveaxis(pieces, 0, dim)
+    shape = pieces.shape
+    return pieces.reshape(*shape[:dim], shape[dim] * shape[dim + 1], *shape[dim + 2 :])
+
+
+def grow_blocks(x, axis):
+    size, mine = (lax.axis_size(axis), lax.axis_index(axis))
+    blocks, stride = (x[None], 1)
+    while stride < size:
+        other = lax.ppermute(blocks, axis, [(i, i ^ stride) for i in range(size)])
+        low = mine & stride == 0
+        blocks = jnp.concatenate([jnp.where(low, blocks, other), jnp.where(low, other, blocks)])
+        stride *= 2
+    return blocks
+
+
+def collect(array, axis, dim):
+    return joined_along(grow_blocks(array, axis), dim)
 
 
 def normalize(values, norm_gain, norm_bias):
@@ -49,7 +70,7 @@
 
 
 def gather_rows(tensor):
-    return lax.all_gather(tensor, "seq", axis=1, tiled=True)
+    return collect(tensor, "seq", 1)
 
 
 def sum_partial(tensor):

time: 675 us -> 735 us (1.089)
  waiting for transfers between devices: 303 us -> 347 us
  other arithmetic: 25.7 us -> 38.5 us
    ppermute x0 -> x4, waiting for transfers between devices: none -> 153 us  [grow_blocks(): other = lax.ppermute(blocks, axis, [(i, i ^ stride) for i in range(size)])]
    all_gather x2 -> x0, waiting for transfers between devices: 108 us -> none  [gather_rows(): return lax.all_gather(tensor, 'seq', axis=1, tiled=True)]
    unnamed x180 -> x192, local copies, waits for them, and re-layouts: 29.5 us -> 35.9 us
    unnamed x12 -> x10, waiting for transfers between devices: 39.9 us -> 40 us
  transfers between devices with their start and end apart: 15 -> 17, of which waited for: 10 -> 12; matrix products, arithmetic and copies ran while one was open for 17% -> 16% of each run, Pallas kernels for 0% -> 0%
where the time goes in v1:
time: 735 us; the launch traced here: 726 us
  waiting for transfers between devices  347 us (47%)
  blocking collectives  142 us (19%)
  matrix products  83.5 us (11%)
  local copies, waits for them, and re-layouts  74.7 us (10%)
  other arithmetic  38.5 us (5%)
  starting transfers between devices  23.3 us (3%)
  between operations  16.7 us (2%)
    ppermute x4, waiting for transfers between devices, grow_blocks(): other = lax.ppermute(blocks, axis, [(i, i ^ stride) for i in range(size)])  153 us
    reduce_scatter x2, waiting for transfers between devices, sum_partial(): lax.psum_scatter(tensor.astype(jnp.bfloat16), 'seq', scatter_dimension=1,...  106 us
    unnamed x2, blocking collectives  50.6 us
    unnamed x10, waiting for transfers between devices  40 us
    unnamed x192, local copies, waits for them, and re-layouts  35.9 us
    all_to_all x2, waiting for transfers between devices, to_heads(): lax.all_to_all(tensor, 'seq', split_axis=2, concat_axis=0, tiled=True)  32.1 us
    all_to_all x2, blocking collectives, to_owners(): return lax.all_to_all(tensor, 'dp', split_axis=0, concat_axis=1, tiled=True)  31.4 us
    all_to_all x1, blocking collectives, to_tokens(): lax.all_to_all(tensor, 'seq', split_axis=0, concat_axis=1, tiled=True)  25.9 us
  transfers between devices with their start and end apart: 17, of which 12 were waited for; matrix products, arithmetic and copies ran while one was open for 16% of the time, Pallas kernels for 0%

profile of v1, /device:TPU:0, one launch (start us, length us, event | category | flops | bytes accessed | tf_op | source)
XLA Modules:
  0.0 726.0 jit_solution(15400388799871182722)
XLA Ops:
  15.9 26.9 %all-reduce.16 = (bf16[768]{0:T(1024)(128)(2,1)S(1)}, bf16[768]{0:T(1024)(128)(2,1)S(1)}, bf16[768]{0:T(1024)(128)(2,1)S(1)}, bf16[768]{0:T(1024)(128)(2,1)S(1)}...) all-reduce(bf16[768]{0:T(1024)(128)(2,1)S(1)} %dynamic-update-slice, ...), channel_id=1, replica_groups=mesh['dp'=8,'seq'=4] {'dp'}, use_global_device_ids=true, to_apply=%add.4 | all-reduce | flops 5376 | bytes 21504
  46.7 4.1 fusion.10
  50.8 3.8 reshape.643
  54.6 3.4 copy.97
  58.0 4.6 all-to-all-start
  65.8 25.9 %all-to-all-done = bf16[1,3,4,192,200]{4,3,1,0,2:T(8,128)(2,1)} async-done(((bf16[1,3,4,192,200]{4,3,1,0,2:T(8,128)(2,1)}), bf16[1,3,4,192,200]{4,3,1,0,2:T(8,128)(2,1)}, u32[]{:S(2)}, u32[]{:S(2)}) %all-to-all-start) | async-done | bytes 921632 | tf_op jit(solution)/shard_map/all_to_all | solution.py:57
  95.7 4.3 convolution_convert_fusion.3
  100.0 3.5 all-to-all-start.1
  108.2 6.5 all-to-all-done.1
  118.6 15.2 %all_to_all.105 = bf16[32,14,768]{2,1,0:T(8,128)(2,1)S(1)} all-to-all(bf16[32,14,768]{2,1,0:T(8,128)(2,1)S(1)} %copy.103), channel_id=1, replica_groups=mesh['dp'=8,'seq'=4] {'dp'}, dimensions={0} | all-to-all | bytes 1376256 | tf_op jit(solution)/shard_map/all_to_all | solution.py:65
  135.0 16.9 %collective-permute-done = bf16[1,4,112,768]{3,1,2,0:T(4,128)(2,1)} collective-permute-done((bf16[1,4,112,768]{3,1,2,0:T(4,128)(2,1)}, bf16[1,4,112,768]{3,1,2,0:T(4,128)(2,1)}, u32[]{:S(2)}, u32[]{:S(2)}) %collective-permute-start) | collective-permute-done | bytes 688160 | tf_op jit(solution)/shard_map/ppermute | solution.py:24
  156.6 60.9 %collective-permute-done.1 = bf16[2,4,112,768]{3,1,2,0:T(4,128)(2,1)} collective-permute-done((bf16[2,4,112,768]{3,1,2,0:T(4,128)(2,1)}, bf16[2,4,112,768]{3,1,2,0:T(4,128)(2,1)}, u32[]{:S(2)}, u32[]{:S(2)}) %collective-permute-start.1) | collective-permute-done | bytes 1376288 | tf_op jit(solution)/shard_map/ppermute | solution.py:24
  217.5 3.0 broadcast_select_fusion.3
  222.6 2.5 copy-done.10
  227.0 3.8 multiply_convert_fusion.1
  232.0 3.1 convolution_convert_fusion
  235.2 52.9 %reduce-scatter.10.cloned.1.call-done = bf16[4,112,768]{2,1,0:T(8,128)(2,1)} async-done(((bf16[4,448,768]{2,1,0:T(8,128)(2,1)}), bf16[4,112,768]{2,1,0:T(8,128)(2,1)}) %reduce-scatter.10.cloned.1.call-update) | async-done | bytes 688144 | tf_op jit(solution)/shard_map/reduce_scatter | solution.py:77
  290.4 4.2 all-to-all-start.3
  294.7 14.8 %all-gather = bf16[8,96,32]{1,2,0:T(8,128)(2,1)S(1)} all-gather(bf16[1,96,32]{1,2,0:T(8,128)(2,1)} %bitcast.320), channel_id=1, replica_groups=mesh['dp'=8,'seq'=4] {'dp'}, dimensions={0}, use_global_device_ids=true | all-gather | bytes 55296 | tf_op jit(solution)/shard_map/all_gather | solution.py:170
  321.3 2.5 fusion.52
  328.4 16.2 %all_to_all.106 = bf16[32,14,768]{2,1,0:T(8,128)(2,1)S(1)} all-to-all(bf16[32,14,768]{2,1,0:T(8,128)(2,1)} %convert_element_type.299), channel_id=1, replica_groups=mesh['dp'=8,'seq'=4] {'dp'}, dimensions={0} | all-to-all | bytes 1376256 | tf_op jit(solution)/shard_map/all_to_all | solution.py:65
  345.7 16.0 %collective-permute-done.2 = bf16[1,4,112,768]{3,1,2,0:T(4,128)(2,1)S(1)} collective-permute-done((bf16[1,4,112,768]{3,1,2,0:T(4,128)(2,1)S(1)}, bf16[1,4,112,768]{3,1,2,0:T(4,128)(2,1)S(1)}, u32[]{:S(2)}, u32[]{:S(2)}) %collective-permute-start.2) | collective-permute-done | bytes 688160 | tf_op jit(solution)/shard_map/ppermute | solution.py:24
  364.9 58.8 %collective-permute-done.3 = bf16[2,4,112,768]{3,1,2,0:T(4,128)(2,1)S(1)} collective-permute-done((bf16[2,4,112,768]{3,1,2,0:T(4,128)(2,1)S(1)}, bf16[2,4,112,768]{3,1,2,0:T(4,128)(2,1)S(1)}, u32[]{:S(2)}, u32[]{:S(2)}) %collective-permute-start.3) | collective-permute-done | bytes 1376288 | tf_op jit(solution)/shard_map/ppermute | solution.py:24
  427.6 2.7 copy-done.28
  430.3 4.0 multiply_convert_fusion
  437.5 3.3 add_convert_fusion
  440.9 53.3 %reduce-scatter.12.cloned.1.call-done = bf16[4,112,768]{2,1,0:T(8,128)(2,1)} async-done(((bf16[4,448,768]{2,1,0:T(8,128)(2,1)}), bf16[4,112,768]{2,1,0:T(8,128)(2,1)}) %reduce-scatter.12.cloned.1.call-update) | async-done | bytes 688144 | tf_op jit(solution)/shard_map/reduce_scatter | solution.py:77
  496.4 3.6 all-to-all-start.5
  502.9 8.6 %all-to-all-done.5 = bf16[4,112,768]{2,0,1:T(4,128)(2,1)S(1)} async-done(((bf16[4,112,768]{2,0,1:T(4,128)(2,1)}), bf16[4,112,768]{2,0,1:T(4,128)(2,1)S(1)}, u32[]{:S(2)}, u32[]{:S(2)}) %all-to-all-start.5) | async-done | bytes 688160 | tf_op jit(solution)/shard_map/all_to_all | solution.py:69
  514.7 2.5 fusion.44
  523.2 3.5 all-to-all-start.6
  526.7 2.8 fusion.14
  529.6 6.3 all-to-all-done.6
  536.6 4.3 convolution_convert_fusion.2
  542.6 4.0 fusion.33
  546.5 4.3 fusion.30
  552.9 25.9 %all_to_all.107 = bf16[4,576,200]{1,2,0:T(8,128)(2,1)} all-to-all(bf16[4,576,200]{1,2,0:T(8,128)(2,1)S(1)} %copy.119), channel_id=1, replica_groups=mesh['dp'=8,'seq'=4] {'seq'}, dimensions={0} | all-to-all | bytes 1843200 | tf_op jit(solution)/shard_map/all_to_all | solution.py:61
  581.6 3.4 copy.123
  585.0 8.0 %copy.133 = f32[768,2304]{1,0:T(8,128)} copy(f32[768,2304]{0,1:T(8,128)} %bitcast.267) | data formatting | bytes 14155776
  593.9 5.9 copy.121
  600.8 6.7 fusion.132
  607.5 4.6 fusion.133
  612.1 4.6 fusion.134
  617.2 3.8 fusion.43
  622.7 38.5 %reduce-scatter.16.cloned.1.call-done = f32[96,2304]{1,0:T(8,128)} async-done(((f32[768,2304]{1,0:T(8,128)}), f32[96,2304]{1,0:T(8,128)}) %reduce-scatter.16.cloned.1.call-update) | async-done | bytes 884752
  664.9 23.7 %all-reduce.15 = (bf16[768]{0:T(1024)(128)(2,1)S(1)}, bf16[768]{0:T(1024)(128)(2,1)S(1)}, bf16[768]{0:T(1024)(128)(2,1)S(1)}, bf16[768]{0:T(1024)(128)(2,1)S(1)}...) all-reduce(f32[768]{0:T(1024)S(1)} %get-tuple-element.62, ...), channel_id=4, replica_groups=mesh['dp'=8,'seq'=4] {'dp'}, use_global_device_ids=true, to_apply=%region_23.24.clone | all-reduce | flops 5376 | bytes 32256
  689.1 19.3 %all-reduce.17 = (bf16[96]{0:T(256)(128)(2,1)S(1)}, bf16[96]{0:T(256)(128)(2,1)S(1)}, bf16[96]{0:T(256)(128)(2,1)S(1)}, bf16[96]{0:T(256)(128)(2,1)S(1)}, bf16[9...) all-reduce(bf16[96]{0:T(256)(128)(2,1)S(1)} %dynamic-slice.34, ...), channel_id=1, replica_groups=mesh['dp'=8,'seq'=4] {'seq'}, use_global_device_ids=true, to_apply=%region_24.25 | all-reduce | flops 3744 | bytes 14976 | tf_op jit(solution)/shard_map/psum | solution.py:359
  712.6 2.5 fusion.47
  (311 shorter events, 105.6 us)
Async XLA Ops:
  7.2 224.9 %copy-start = (bf16[4,512,768]{2,1,0:T(8,128)(2,1)S(1)}, bf16[4,512,768]{2,1,0:T(8,128)(2,1)}, u32[]{:S(2)}) copy-start(bf16[4,512,768]{2,1,0:T(8,128)(2,1)} %param.30) | copy-start | bytes 9437188
  7.2 39.5 %all-gather.4.cloned.1.call-start = ((), (), s32[]{:S(2)}) async-start(), calls=%async_computation.13 | async-start | bytes 3981312 | tf_op jit(solution)/shard_map/all_gather | solution.py:163
  42.8 7.9 %copy-start.48 = (f32[768]{0:T(1024)}, f32[768]{0:T(1024)S(1)}, u32[]{:S(2)}) copy-start(f32[768]{0:T(1024)S(1)} %convert_element_type.274) | copy-start | bytes 9220
  44.1 6.7 copy-start.50
  54.6 8.8 %copy-start.47 = (s32[1,200,2]{1,2,0:T(2,128)S(1)}, s32[1,200,2]{1,2,0:T(2,128)}, u32[]{:S(2)}) copy-start(s32[1,200,2]{1,2,0:T(2,128)} %param.31) | copy-start | bytes 4804
  54.6 9.4 %copy-start.77 = (s32[4,200]{1,0:T(4,128)S(1)}, s32[4,200]{1,0:T(4,128)}, u32[]{:S(2)}) copy-start(s32[4,200]{1,0:T(4,128)} %param.32) | copy-start | bytes 9604
  58.0 33.6 %all-to-all-start = ((bf16[1,3,4,192,200]{4,3,1,0,2:T(8,128)(2,1)}), bf16[1,3,4,192,200]{4,3,1,0,2:T(8,128)(2,1)}, u32[]{:S(2)}, u32[]{:S(2)}) async-start(bf16[1,3,4,192,200]{4,3,1,0,2:T(8,128)(2,1)} %copy.97), calls=%async_computation | async-start | bytes 2359296 | tf_op jit(solution)/shard_map/all_to_all | solution.py:57
  62.6 45.6 %all-gather.6.cloned.1.call-start = ((), (), s32[]{:S(2)}) async-start(), calls=%async_computation.14 | async-start | bytes 1327104 | tf_op jit(solution)/shard_map/all_gather | solution.py:166
  64.0 31.7 %copy-start.78 = (f32[4,200]{1,0:T(4,128)}, f32[4,200]{1,0:T(4,128)S(1)}, u32[]{:S(2)}) copy-start(f32[4,200]{1,0:T(4,128)S(1)} %convert_element_type.280) | copy-start | bytes 9604
  93.0 7.0 copy-start.38
  100.0 14.7 %all-to-all-start.1 = ((bf16[4,192,200]{2,1,0:T(8,128)(2,1)}), bf16[4,192,200]{2,1,0:T(8,128)(2,1)S(1)}, u32[]{:S(2)}, u32[]{:S(2)}) async-start(bf16[4,192,200]{2,1,0:T(8,128)(2,1)} %bitcast.304), calls=%async_computation.1 | async-start | bytes 786432 | tf_op jit(solution)/shard_map/all_to_all | solution.py:61
  103.5 184.6 %reduce-scatter.10.cloned.1.call-start = ((), (), s32[]{:S(2)}) async-start(), calls=%async_computation.15 | async-start | bytes 3440640 | tf_op jit(solution)/shard_map/reduce_scatter | solution.py:77
  116.7 17.2 %copy-start.8 = (f32[1,200,768]{2,1,0:T(8,128)}, f32[1,200,768]{2,1,0:T(8,128)S(1)}, u32[]{:S(2)}) copy-start(f32[1,200,768]{2,1,0:T(8,128)S(1)} %get-tuple-element.120) | copy-start | bytes 1843204
  135.0 16.9 %collective-permute-start = (bf16[1,4,112,768]{3,1,2,0:T(4,128)(2,1)}, bf16[1,4,112,768]{3,1,2,0:T(4,128)(2,1)}, u32[]{:S(2)}, u32[]{:S(2)}) collective-permute-start(bf16[1,4,112,768]{3,1,2,0:T(4,128)(2,1)} %bitcast.31), channel_id=1, source_target_pairs={{0,1},{1,0},{2,3},{3,2},{4,5},{5,4},{6,7},{7,6},{8,9},{9,8},{10,11... | collective-permute-start | bytes 2064392 | tf_op jit(solution)/shard_map/ppermute | solution.py:24
  156.3 61.2 %collective-permute-start.1 = (bf16[2,4,112,768]{3,1,2,0:T(4,128)(2,1)}, bf16[2,4,112,768]{3,1,2,0:T(4,128)(2,1)}, u32[]{:S(2)}, u32[]{:S(2)}) collective-permute-start(bf16[2,4,112,768]{3,1,2,0:T(4,128)(2,1)} %pad_maximum_fusion), channel_id=1, source_target_pairs={{0,2},{1,3},{2,0},{3,1},{4,6},{5,7},{6,4},{7,5},{8,10},{9,11},{10,... | collective-permute-start | bytes 4128776 | tf_op jit(solution)/shard_map/ppermute | solution.py:24
  290.4 24.3 %all-to-all-start.3 = ((bf16[4,112,768]{2,0,1:T(4,128)(2,1)}), bf16[4,112,768]{2,0,1:T(4,128)(2,1)}, u32[]{:S(2)}, u32[]{:S(2)}) async-start(bf16[4,112,768]{2,0,1:T(4,128)(2,1)} %copy.106), calls=%async_computation.4 | async-start | bytes 1376256 | tf_op jit(solution)/shard_map/all_to_all | solution.py:69
  294.6 199.5 %reduce-scatter.12.cloned.1.call-start = ((), (), s32[]{:S(2)}) async-start(), calls=%async_computation.16 | async-start | bytes 3440640 | tf_op jit(solution)/shard_map/reduce_scatter | solution.py:77
  316.8 7.6 %copy-start.55 = (s32[1,200,1]{1,2,0:T(1,128)S(1)}, s32[1,200,1]{1,2,0:T(1,128)}, u32[]{:S(2)}) copy-start(s32[1,200,1]{1,2,0:T(1,128)} %get-tuple-element.115) | copy-start | bytes 2404
  345.0 16.7 %collective-permute-start.2 = (bf16[1,4,112,768]{3,1,2,0:T(4,128)(2,1)S(1)}, bf16[1,4,112,768]{3,1,2,0:T(4,128)(2,1)S(1)}, u32[]{:S(2)}, u32[]{:S(2)}) collective-permute-start(bf16[1,4,112,768]{3,1,2,0:T(4,128)(2,1)S(1)} %bitcast.288), channel_id=1, source_target_pairs={{0,1},{1,0},{2,3},{3,2},{4,5},{5,4},{6,7},{7,6},{8,9},{9,8},{10,11... | collective-permute-start | bytes 2064392 | tf_op jit(solution)/shard_map/ppermute | solution.py:24
  362.7 60.9 %collective-permute-start.3 = (bf16[2,4,112,768]{3,1,2,0:T(4,128)(2,1)S(1)}, bf16[2,4,112,768]{3,1,2,0:T(4,128)(2,1)S(1)}, u32[]{:S(2)}, u32[]{:S(2)}) collective-permute-start(bf16[2,4,112,768]{3,1,2,0:T(4,128)(2,1)S(1)} %pad_maximum_fusion.1), channel_id=1, source_target_pairs={{0,2},{1,3},{2,0},{3,1},{4,6},{5,7},{6,4},{7,5},{8,10},{9,11},{10,... | collective-permute-start | bytes 4128776 | tf_op jit(solution)/shard_map/ppermute | solution.py:24
  440.8 59.4 %copy-start.41 = (f32[1,200,2,32]{1,3,2,0:T(8,128)S(1)}, f32[1,200,2,32]{1,3,2,0:T(8,128)}, u32[]{:S(2)}) copy-start(f32[1,200,2,32]{1,3,2,0:T(8,128)} %convert_convert_fusion) | copy-start | bytes 153604
  440.8 59.4 %copy-start.45 = (f32[200,32]{0,1:T(8,128)S(1)}, f32[200,32]{0,1:T(8,128)}, u32[]{:S(2)}) copy-start(f32[200,32]{0,1:T(8,128)} %get-tuple-element.125) | copy-start | bytes 76804
  440.8 59.4 %copy-start.71 = (f32[200]{0:T(256)S(1)}, f32[200]{0:T(256)}, u32[]{:S(2)}) copy-start(f32[200]{0:T(256)} %get-tuple-element.124) | copy-start | bytes 2404
  440.8 59.4 %copy-start.73 = (f32[200]{0:T(256)S(1)}, f32[200]{0:T(256)}, u32[]{:S(2)}) copy-start(f32[200]{0:T(256)} %copy-done.72) | copy-start | bytes 2404
  440.8 59.4 %copy-start.75 = (f32[200]{0:T(256)S(1)}, f32[200]{0:T(256)}, u32[]{:S(2)}) copy-start(f32[200]{0:T(256)} %copy-done.74) | copy-start | bytes 2404
  440.8 59.4 %copy-start.80 = (f32[200]{0:T(256)S(1)}, f32[200]{0:T(256)}, u32[]{:S(2)}) copy-start(f32[200]{0:T(256)} %get-tuple-element.72) | copy-start | bytes 2404
  440.8 59.5 %copy-start.32 = (bf16[1,200,768]{2,1,0:T(8,128)(2,1)S(1)}, bf16[1,200,768]{2,1,0:T(8,128)(2,1)}, u32[]{:S(2)}) copy-start(bf16[1,200,768]{2,1,0:T(8,128)(2,1)} %copy-done.31) | copy-start | bytes 921604
  440.8 61.0 %copy-start.42 = (bf16[768,32]{0,1:T(8,128)(2,1)S(1)}, bf16[768,32]{0,1:T(8,128)(2,1)}, u32[]{:S(2)}) copy-start(bf16[768,32]{0,1:T(8,128)(2,1)} %reshape.685) | copy-start | bytes 147460
  496.4 15.1 %all-to-all-start.5 = ((bf16[4,112,768]{2,0,1:T(4,128)(2,1)}), bf16[4,112,768]{2,0,1:T(4,128)(2,1)S(1)}, u32[]{:S(2)}, u32[]{:S(2)}) async-start(bf16[4,112,768]{2,0,1:T(4,128)(2,1)} %copy.110), calls=%async_computation.7 | async-start | bytes 1376256 | tf_op jit(solution)/shard_map/all_to_all | solution.py:69
  500.1 14.6 %copy-start.9 = (f32[1,200,768]{2,1,0:T(8,128)S(1)}, f32[1,200,768]{2,1,0:T(8,128)}, u32[]{:S(2)}) copy-start(f32[1,200,768]{2,1,0:T(8,128)} %copy-done.8) | copy-start | bytes 1843204
  500.1 14.6 %copy-start.53 = (f32[200]{0:T(256)S(1)}, f32[200]{0:T(256)}, u32[]{:S(2)}) copy-start(f32[200]{0:T(256)} %copy-done.52) | copy-start | bytes 2404
  500.1 14.6 %copy-start.56 = (s32[1,200,1]{1,2,0:T(1,128)S(1)}, s32[1,200,1]{1,2,0:T(1,128)}, u32[]{:S(2)}) copy-start(s32[1,200,1]{1,2,0:T(1,128)} %get-tuple-element.115) | copy-start | bytes 2404
  500.1 14.6 %copy-start.63 = (s32[1,200,1]{1,2,0:T(1,128)S(1)}, s32[1,200,1]{1,2,0:T(1,128)}, u32[]{:S(2)}) copy-start(s32[1,200,1]{1,2,0:T(1,128)} %get-tuple-element.116) | copy-start | bytes 2404
  500.1 99.8 %reduce-scatter.18.cloned.1.call-start = ((), (), s32[]{:S(2)}) async-start(), calls=%async_computation.19 | async-start | bytes 442368
  501.4 119.7 %reduce-scatter.14.cloned.1.call-start = ((), (), s32[]{:S(2)}) async-start(), calls=%async_computation.17 | async-start | bytes 2654208 | tf_op jit(solution)/shard_map/reduce_scatter | solution.py:341
  523.2 12.6 %all-to-all-start.6 = ((bf16[1,1,4,192,200]{4,3,1,0,2:T(8,128)(2,1)}), bf16[1,1,4,192,200]{4,3,1,0,2:T(8,128)(2,1)S(1)}, u32[]{:S(2)}, u32[]{:S(2)}) async-start(bf16[1,1,4,192,200]{4,3,1,0,2:T(8,128)(2,1)} %bitcast.58), calls=%async_computation.8 | async-start | bytes 786432 | tf_op jit(solution)/shard_map/all_to_all | solution.py:57
  526.6 134.6 %reduce-scatter.16.cloned.1.call-start = ((), (), s32[]{:S(2)}) async-start(), calls=%async_computation.18 | async-start | bytes 7962624
  552.9 27.5 %copy-start.6 = (f32[1,200,768]{2,1,0:T(8,128)S(1)}, f32[1,200,768]{2,1,0:T(8,128)}, u32[]{:S(2)}) copy-start(f32[1,200,768]{2,1,0:T(8,128)} %param.17) | copy-start | bytes 1843204
  552.9 27.5 %copy-start.49 = (f32[768]{0:T(1024)S(1)}, f32[768]{0:T(1024)}, u32[]{:S(2)}) copy-start(f32[768]{0:T(1024)} %copy-done.48) | copy-start | bytes 9220
  552.9 27.5 %copy-start.51 = (f32[200]{0:T(256)S(1)}, f32[200]{0:T(256)}, u32[]{:S(2)}) copy-start(f32[200]{0:T(256)} %copy-done.50) | copy-start | bytes 2404
  552.9 27.5 %copy-start.65 = (f32[200]{0:T(256)S(1)}, f32[200]{0:T(256)}, u32[]{:S(2)}) copy-start(f32[200]{0:T(256)} %copy-done.64) | copy-start | bytes 2404
  593.1 122.1 %all-reduce.21.cloned.1.call-start = ((), (), s32[]{:S(2)}) async-start(), calls=%async_computation.20 | async-start | bytes 1474560 | tf_op jit(solution)/shard_map/psum | solution.py:361
  593.9 6.8 copy-start.3
  600.8 6.7 copy-start.18
  621.0 43.8 %copy-start.57 = (f32[768]{0:T(1024)S(1)}, f32[768]{0:T(1024)}, u32[]{:S(2)}) copy-start(f32[768]{0:T(1024)} %get-tuple-element.60) | copy-start | bytes 9220
  621.0 43.8 %copy-start.58 = (f32[768]{0:T(1024)S(1)}, f32[768]{0:T(1024)}, u32[]{:S(2)}) copy-start(f32[768]{0:T(1024)} %get-tuple-element.66) | copy-start | bytes 9220
  621.0 43.8 %copy-start.59 = (f32[768]{0:T(1024)S(1)}, f32[768]{0:T(1024)}, u32[]{:S(2)}) copy-start(f32[768]{0:T(1024)} %get-tuple-element.99) | copy-start | bytes 9220
  663.5 55.5 %copy-start.1 = (bf16[4,512,768]{2,1,0:T(8,128)(2,1)S(1)}, bf16[4,512,768]{2,1,0:T(8,128)(2,1)}, u32[]{:S(2)}) copy-start(bf16[4,512,768]{2,1,0:T(8,128)(2,1)} %param.30) | copy-start | bytes 9437188
  (51 other events, 160.3 us)
Sparse Core Ops, SparseCore 0:
  9.9 36.7 all-gather.3
  65.3 24.3 all-gather.5
  235.3 52.7 reduce-scatter.9
  441.0 53.1 reduce-scatter.11
  503.7 34.0 reduce-scatter.17
  541.0 42.3 reduce-scatter.13
  593.2 67.9 reduce-scatter.15
  664.2 43.1 all-reduce.20
